TPU v7x, 32 devices: a whole 2x2x4 slice. The times are simulated.
32 devices in a mesh: brick: 8 (over z, x), group: 4 (over y, core).
Axes of the slice: x: 2, y: 2, z: 4, core: 2. Of those that a mesh axis runs over, the one named last changes fastest.
Arguments:
- features: bfloat16 [32768, 96], P(('brick', 'group')), may hold values from -6 to 6
- order: int32 [32768], P(('brick', 'group')), may hold values from 0 to 1023, as said below
- face_list: int32 [8192], P(('brick', 'group')), may hold values from 0 to 1023, as said below
- face_count: int32 [64], P(('brick', 'group')), may hold values from 32 to 128, as said below
- kernel_map: int32 [27, 32768], P(None, ('brick', 'group')), may hold values from 0 to 1280, as said below
- weight: bfloat16 [27, 96, 256], replicated, may hold values from -0.15625 to 0.15625
- bias: float32 [256], replicated, may hold values from -3 to 3
- cotangent: bfloat16 [32768, 256], P(('brick', 'group')), may hold values from -6 to 6
Outputs:
- output: bfloat16 [32768, 256], P(('brick', 'group'))
- grad_in: bfloat16 [32768, 96], P(('brick', 'group'))
- weight_grad: float32 [27, 96, 256], replicated
Inputs may be any that keep to these rules, and one draw needn't show every extreme that they name: `order`: each device's 1024 entries are a permutation of 0 .. 1023. `face_list`: rows of the device's own brick. `face_count`: some list is full in every draw. `kernel_map`: the value 1024 + 2 * 128 names the zero row; offset 27 // 2 maps every voxel i to row i.
All inputs are finite; a program needn't handle non-finite values.
Results may differ from a plain program's by a relative error of at most 0.012.
Values may be sent and summed in bfloat16 or wider, within the bound.
No kernel may reach another device: no remote copies, remote signals or barrier semaphores. Data moves between devices by JAX's collectives and lax.ppermute only.
A program may use at most 64 MiB of HBM per device.

v0:
```python
import math
import jax
import jax.numpy as jnp
from jax import lax
from jax.sharding import PartitionSpec as P


def from_behind(array, axis, by):
    size = lax.axis_size(axis)
    pairs = [(i, i + by) for i in range(size) if 0 <= i + by < size]
    return lax.ppermute(array, axis, pairs)


def one_hot_rows(index, width):
    columns = jnp.arange(width, dtype=jnp.int32)
    return (index[:, None] == columns[None, :]).astype(jnp.bfloat16)


def pick_rows(selector, values):
    return jnp.dot(selector, values, preferred_element_type=jnp.float32).astype(jnp.bfloat16)


def spread_rows(selector, values):
    high_part = values.astype(jnp.bfloat16)
    low_part = (values - high_part.astype(jnp.float32)).astype(jnp.bfloat16)
    dims = (((0,), (0,)), ((), ()))
    first = lax.dot_general(selector, high_part, dims, preferred_element_type=jnp.float32)
    second = lax.dot_general(selector, low_part, dims, preferred_element_type=jnp.float32)
    return first + second


def on_device(features, order, face_list, face_count, kernel_map, weight, bias, cotangent):
    rows_here = features.shape[0]
    face_slots = face_list.shape[0] // 2
    order_pick = one_hot_rows(order, rows_here)
    sent_rows = pick_rows(order_pick, features)
    local_rows = lax.all_to_all(sent_rows, "brick", split_axis=0, concat_axis=0, tiled=True)
    slots = jnp.arange(face_slots, dtype=jnp.int32)
    lower_keep = (slots < face_count[0]).astype(jnp.bfloat16)[:, None]
    upper_keep = (slots < face_count[1]).astype(jnp.bfloat16)[:, None]
    lower_pick = one_hot_rows(face_list[:face_slots], rows_here) * lower_keep
    upper_pick = one_hot_rows(face_list[face_slots:], rows_here) * upper_keep
    lower_rows = pick_rows(lower_pick, local_rows)
    upper_rows = pick_rows(upper_pick, local_rows)
    prev_upper = from_behind(upper_rows, "brick", 1)
    next_lower = from_behind(lower_rows, "brick", -1)
    zero_row = jnp.zeros((1, local_rows.shape[1]), jnp.bfloat16)
    extended = jnp.concatenate([local_rows, prev_upper, next_lower, zero_row], 0)
    ext_count = extended.shape[0]

    def forward(summed, operands):
        map_row, kernel = operands
        gathered = pick_rows(one_hot_rows(map_row, ext_count), extended)
        return (summed + jnp.dot(gathered, kernel, preferred_element_type=jnp.float32), None)

    start = jnp.zeros((rows_here, weight.shape[2]), jnp.float32)
    pre, _ = lax.scan(forward, start, (kernel_map, weight))
    pre = pre + bias
    output = jnp.maximum(pre, 0.0).astype(jnp.bfloat16)
    pre_grad = jnp.where(pre > 0, cotangent, jnp.zeros_like(cotangent))

    def offset_grads(ext_grad, map_row, kernel):
        selector = one_hot_rows(map_row, ext_count)
        gathered = pick_rows(selector, extended)
        kernel_grad = lax.dot_general(
            gathered, pre_grad, (((0,), (0,)), ((), ())), preferred_element_type=jnp.float32
        )
        contrib = lax.dot_general(
            pre_grad, kernel, (((1,), (1,)), ((), ())), preferred_element_type=jnp.float32
        )
        return (ext_grad + spread_rows(selector, contrib), kernel_grad)

    zeros_grad = jnp.zeros((ext_count, extended.shape[1]), jnp.float32)

    def backward(ext_grad, operands):
        map_row, kernel = operands
        return offset_grads(ext_grad, map_row, kernel)

    ext_grad, kernel_grads = lax.scan(backward, zeros_grad, (kernel_map, weight))
    weight_sum = lax.psum(kernel_grads, ("brick", "group"))
    to_prev = ext_grad[rows_here : rows_here + face_slots]
    to_next = ext_grad[rows_here + face_slots : rows_here + 2 * face_slots]
    from_prev = from_behind(to_next.astype(jnp.bfloat16), "brick", 1).astype(to_next.dtype)
    from_next = from_behind(to_prev.astype(jnp.bfloat16), "brick", -1).astype(to_prev.dtype)
    local_grad = (
        ext_grad[:rows_here]
        + spread_rows(lower_pick, from_prev)
        + spread_rows(upper_pick, from_next)
    )
    brick_grad = local_grad.astype(jnp.bfloat16)
    returned = lax.all_to_all(brick_grad, "brick", split_axis=0, concat_axis=0, tiled=True)
    grad_in = lax.dot_general(
        order_pick, returned, (((0,), (0,)), ((), ())), preferred_element_type=jnp.float32
    ).astype(jnp.bfloat16)
    voxel_total = lax.axis_size("brick") * lax.axis_size("group") * rows_here
    weight_grad = weight_sum * jnp.float32(1.0 / math.sqrt(voxel_total))
    return (output, grad_in, weight_grad)


def solution(mesh):
    return jax.shard_map(
        on_device,
        mesh=mesh,
        in_specs=(
            P(("brick", "group"), None),
            P(("brick", "group")),
            P(("brick", "group")),
            P(("brick", "group")),
            P(None, ("brick", "group")),
            P(),
            P(),
            P(("brick", "group"), None),
        ),
        out_specs=(P(("brick", "group"), None), P(("brick", "group"), None), P()),
        check_vma=False,
    )
```

profile of v0, /device:TPU:0, one launch (start us, length us, event | category | flops | bytes accessed | tf_op | source)
XLA Modules:
  0.0 454.1 jit_solution(2190139345262719592)
XLA Ops:
  10.5 7.2 %all-to-all-start = ((bf16[8,128,96]{1,2,0:T(8,128)(2,1)}), bf16[8,128,96]{1,2,0:T(8,128)(2,1)S(1)}, u32[]{:S(2)}, u32[]{:S(2)}) async-start(bf16[8,128,96]{1,2,0:T(8,128)(2,1)} %bitcast.53), calls=%async_computation | async-start | bytes 393216 | tf_op jit(solution)/shard_map/all_to_all | solution.py:37
  21.3 4.4 all-to-all-done
  26.0 3.0 collective-permute-start
  30.6 4.4 collective-permute-done.1
  35.3 92.4 %while.24 = (s32[]{:T(128)}, f32[1024,256]{1,0:T(8,128)S(1)}, s32[27,1024]{1,0:T(8,128)}, bf16[1281,96]{1,0:T(8,128)(2,1)S(1)}, bf16[27,96,256]{2,1,0:T(8,128)(2,1)}, /*index=5*/s32[]{:T(128)}, s32[]{:T(128)}) while((s32[]{:T(128)}, f32[1024,256]{1,0:T(8,128)S(1)}, s32[27,1024]{1,0:T(8,128)}, bf16[1281,96]{1,0:T(8,128)(2,1)S(1)}, ...), condition=%wide.region_1.2_spmd.clone, body=%wide.region_0.1_spmd.clone.sunk | while | flops 304120832 | bytes 2404647 | solution.py:57
  36.2 2.6 convolution_add_fusion.4
  39.6 2.6 convolution_add_fusion.4
  43.0 2.6 convolution_add_fusion.4
  46.4 2.6 convolution_add_fusion.4
  49.8 2.6 convolution_add_fusion.4
  53.3 2.6 convolution_add_fusion.4
  56.7 2.6 convolution_add_fusion.4
  60.1 2.6 convolution_add_fusion.4
  63.5 2.6 convolution_add_fusion.4
  66.9 2.6 convolution_add_fusion.4
  70.4 2.6 convolution_add_fusion.4
  73.8 2.6 convolution_add_fusion.4
  77.2 2.6 convolution_add_fusion.4
  80.6 2.6 convolution_add_fusion.4
  84.0 2.6 convolution_add_fusion.4
  87.5 2.6 convolution_add_fusion.4
  90.9 2.6 convolution_add_fusion.4
  94.3 2.6 convolution_add_fusion.4
  97.7 2.6 convolution_add_fusion.4
  101.1 2.6 convolution_add_fusion.4
  104.5 2.6 convolution_add_fusion.4
  108.0 2.6 convolution_add_fusion.4
  111.4 2.6 convolution_add_fusion.4
  114.8 2.6 convolution_add_fusion.4
  118.2 2.6 convolution_add_fusion.4
  121.6 2.6 convolution_add_fusion.4
  125.1 2.6 convolution_add_fusion.4
  127.9 176.2 %while.25 = (s32[]{:T(128)}, f32[1281,96]{0,1:T(8,128)S(1)}, f32[27,96,256]{2,1,0:T(8,128)}, s32[27,1024]{1,0:T(8,128)}, bf16[27,96,256]{2,1,0:T(8,128)(2,1)}, /...) while((s32[]{:T(128)}, f32[1281,96]{0,1:T(8,128)S(1)}, ...), condition=%wide.region_3.4_spmd.clone, body=%wide.region_2.3_spmd.clone.sunk | while | flops 861121792 | bytes 4609851 | solution.py:79
  132.3 2.1 fusion.103
  138.9 2.1 fusion.103
  145.4 2.1 fusion.103
  151.9 2.1 fusion.103
  158.4 2.1 fusion.103
  165.0 2.1 fusion.103
  171.5 2.1 fusion.103
  178.0 2.1 fusion.103
  191.1 2.1 fusion.103
  197.6 2.1 fusion.103
  305.5 4.5 %collective-permute-start.2 = (bf16[128,96]{0,1:T(8,128)(2,1)S(1)}, bf16[128,96]{0,1:T(8,128)(2,1)S(1)}, u32[]{:S(2)}, u32[]{:S(2)}) collective-permute-start(bf16[128,96]{0,1:T(8,128)(2,1)S(1)} %get-tuple-element.149), channel_id=1, source_target_pairs={{0,4},{4,8},{8,12},{12,16},{16,20},{20,24},{24,28},{1,5},{5,9},{9,... | collective-permute-start | bytes 73736 | tf_op jit(solution)/shard_map/ppermute | solution.py:11
  313.2 6.1 %all-to-all-start.1 = ((bf16[8,128,96]{1,2,0:T(8,128)(2,1)}), bf16[8,128,96]{1,2,0:T(8,128)(2,1)S(1)}, u32[]{:S(2)}, u32[]{:S(2)}) async-start(bf16[8,128,96]{1,2,0:T(8,128)(2,1)} %bitcast.52), calls=%async_computation.1 | async-start | bytes 393216 | tf_op jit(solution)/shard_map/all_to_all | solution.py:91
  320.1 8.6 %all-to-all-done.1 = bf16[8,128,96]{1,2,0:T(8,128)(2,1)S(1)} async-done(((bf16[8,128,96]{1,2,0:T(8,128)(2,1)}), bf16[8,128,96]{1,2,0:T(8,128)(2,1)S(1)}, u32[]{:S(2)}, u32[]{:S(2)}) %all-to-all-start.1) | async-done | bytes 196640 | tf_op jit(solution)/shard_map/all_to_all | solution.py:91
  330.3 113.4 %all-reduce.2.cloned.1.call-done = f32[27,96,256]{2,1,0:T(8,128)} async-done(((f32[27,96,256]{2,1,0:T(8,128)}), f32[27,96,256]{2,1,0:T(8,128)}) %all-reduce.2.cloned.1.call-update) | async-done | bytes 2654224 | tf_op jit(solution)/shard_map/psum | solution.py:80
  443.7 3.6 broadcast_multiply_fusion
  (192 shorter events, 191.4 us)
Async XLA Ops:
  7.2 0.9 copy-start
  10.5 15.2 %all-to-all-start = ((bf16[8,128,96]{1,2,0:T(8,128)(2,1)}), bf16[8,128,96]{1,2,0:T(8,128)(2,1)S(1)}, u32[]{:S(2)}, u32[]{:S(2)}) async-start(bf16[8,128,96]{1,2,0:T(8,128)(2,1)} %bitcast.53), calls=%async_computation | async-start | bytes 393216 | tf_op jit(solution)/shard_map/all_to_all | solution.py:37
  17.8 425.9 %all-reduce.2.cloned.1.call-start = ((), (), s32[]{:S(2)}) async-start(), calls=%async_computation.2 | async-start | bytes 5308416 | tf_op jit(solution)/shard_map/psum | solution.py:80
  26.0 4.6 %collective-permute-start = (bf16[128,96]{0,1:T(8,128)(2,1)S(1)}, bf16[128,96]{0,1:T(8,128)(2,1)S(1)}, u32[]{:S(2)}, u32[]{:S(2)}) collective-permute-start(bf16[128,96]{0,1:T(8,128)(2,1)S(1)} %convolution_convert_fusion.1), channel_id=1, source_target_pairs={{0,4},{4,8},{8,12},{12,16},{16,20},{20,24},{24,28},{1,5},{5,9},{9,... | collective-permute-start | bytes 73736 | tf_op jit(solution)/shard_map/ppermute | solution.py:11
  29.3 5.7 %collective-permute-start.1 = (bf16[128,96]{0,1:T(8,128)(2,1)S(1)}, bf16[128,96]{0,1:T(8,128)(2,1)S(1)}, u32[]{:S(2)}, u32[]{:S(2)}) collective-permute-start(bf16[128,96]{0,1:T(8,128)(2,1)S(1)} %convolution_convert_fusion), channel_id=1, source_target_pairs={{4,0},{8,4},{12,8},{16,12},{20,16},{24,20},{28,24},{5,1},{9,5},{13... | collective-permute-start | bytes 73736 | tf_op jit(solution)/shard_map/ppermute | solution.py:11
  35.3 92.4 %copy-start.1 = (bf16[1024,256]{1,0:T(8,128)(2,1)S(1)}, bf16[1024,256]{1,0:T(8,128)(2,1)}, u32[]{:S(2)}) copy-start(bf16[1024,256]{1,0:T(8,128)(2,1)} %param.19) | copy-start | bytes 1572868
  35.3 92.4 %copy-start.2 = (f32[256]{0:T(256)S(1)}, f32[256]{0:T(256)}, u32[]{:S(2)}) copy-start(f32[256]{0:T(256)} %param.18) | copy-start | bytes 3076
  304.2 5.9 %collective-permute-start.3 = (bf16[128,96]{0,1:T(8,128)(2,1)S(1)}, bf16[128,96]{0,1:T(8,128)(2,1)S(1)}, u32[]{:S(2)}, u32[]{:S(2)}) collective-permute-start(bf16[128,96]{0,1:T(8,128)(2,1)S(1)} %get-tuple-element.150), channel_id=1, source_target_pairs={{4,0},{8,4},{12,8},{16,12},{20,16},{24,20},{28,24},{5,1},{9,5},{13... | collective-permute-start | bytes 73736 | tf_op jit(solution)/shard_map/ppermute | solution.py:11
  305.5 6.1 %collective-permute-start.2 = (bf16[128,96]{0,1:T(8,128)(2,1)S(1)}, bf16[128,96]{0,1:T(8,128)(2,1)S(1)}, u32[]{:S(2)}, u32[]{:S(2)}) collective-permute-start(bf16[128,96]{0,1:T(8,128)(2,1)S(1)} %get-tuple-element.149), channel_id=1, source_target_pairs={{0,4},{4,8},{8,12},{12,16},{16,20},{20,24},{24,28},{1,5},{5,9},{9,... | collective-permute-start | bytes 73736 | tf_op jit(solution)/shard_map/ppermute | solution.py:11
  310.4 18.4 %copy-start.3 = (s32[1024]{0:T(1024)S(1)}, s32[1024]{0:T(1024)}, u32[]{:S(2)}) copy-start(s32[1024]{0:T(1024)} %param.13) | copy-start | bytes 12292
  313.2 15.6 %all-to-all-start.1 = ((bf16[8,128,96]{1,2,0:T(8,128)(2,1)}), bf16[8,128,96]{1,2,0:T(8,128)(2,1)S(1)}, u32[]{:S(2)}, u32[]{:S(2)}) async-start(bf16[8,128,96]{1,2,0:T(8,128)(2,1)} %bitcast.52), calls=%async_computation.1 | async-start | bytes 393216 | tf_op jit(solution)/shard_map/all_to_all | solution.py:91
Sparse Core Ops, SparseCore 0:
  305.6 138.0 all-reduce.1
where the time goes:
time: 461 us; the launch traced here: 454 us
  matrix products  231 us (50%)
  waiting for transfers between devices  132 us (29%)
  local copies, waits for them, and re-layouts  46.2 us (10%)
  starting transfers between devices  23.5 us (5%)
  between operations  14.3 us (3%)
  other arithmetic  6.1 us (1%)
    psum x1, waiting for transfers between devices, on_device(): weight_sum = lax.psum(kernel_grads, ('brick', 'group'))  113 us
    dot_general x27, matrix products, forward(): jnp.dot(gathered, kernel, preferred_element_type=jnp.float32)  70.8 us
    dot_general x27, matrix products, offset_grads(): lax.dot_general(gathered, pre_grad, (((0,), (0,)), ((), ())), preferred_e...  57.3 us
    dynamic_slice x54, local copies, waits for them, and re-layouts, on_device(): pre, _ = lax.scan(forward, start, (kernel_map, weight))  41.5 us
    dot_general x29, matrix products, spread_rows(): lax.dot_general(selector, high_part, dims, preferred_element_type=jnp.flo...  35.7 us
    dot_general x29, matrix products, spread_rows(): lax.dot_general(selector, low_part, dims, preferred_element_type=jnp.floa...  34.1 us
    dot_general x27, matrix products, offset_grads(): lax.dot_general(pre_grad, kernel, (((1,), (1,)), ((), ())), preferred_ele...  29.2 us
    ppermute x4, starting transfers between devices, from_behind(): return lax.ppermute(array, axis, pairs)  10.1 us
  transfers between devices with their start and end apart: 7, of which 5 were waited for; matrix products, arithmetic and copies ran while one was open for 2% of the time, Pallas kernels for 0%

commit v1 on v0

--- a/solution.py
+++ b/solution.py
@@ -77,7 +77,7 @@
         return offset_grads(ext_grad, map_row, kernel)
 
     ext_grad, kernel_grads = lax.scan(backward, zeros_grad, (kernel_map, weight))
-    weight_sum = lax.psum(kernel_grads, ("brick", "group"))
+    weight_sum = lax.psum(lax.psum(kernel_grads, "group"), "brick")
     to_prev = ext_grad[rows_here : rows_here + face_slots]
     to_next = ext_grad[rows_here + face_slots : rows_here + 2 * face_slots]
     from_prev = from_behind(to_next.astype(jnp.bfloat16), "brick", 1).astype(to_next.dtype)

time: 461 us -> 505 us (1.095)
  waiting for transfers between devices: 132 us -> 175 us
    psum x1 -> x2, waiting for transfers between devices: 113 us -> 152 us  [on_device(): weight_sum = lax.psum(lax.psum(kernel_grads, 'group'), 'brick')]
  transfers between devices with their start and end apart: 7 -> 8, of which waited for: 5 -> 6; matrix products, arithmetic and copies ran while one was open for 2% -> 2% of each run, Pallas kernels for 0% -> 0%
where the time goes in v1:
time: 505 us; the launch traced here: 498 us
  matrix products  231 us (46%)
  waiting for transfers between devices  175 us (35%)
  local copies, waits for them, and re-layouts  46.2 us (9%)
  starting transfers between devices  24.7 us (5%)
  between operations  14.3 us (3%)
  other arithmetic  6.1 us (1%)
    psum x2, waiting for transfers between devices, on_device(): weight_sum = lax.psum(lax.psum(kernel_grads, 'group'), 'brick')  152 us
    dot_general x27, matrix products, forward(): jnp.dot(gathered, kernel, preferred_element_type=jnp.float32)  70.8 us
    dot_general x27, matrix products, offset_grads(): lax.dot_general(gathered, pre_grad, (((0,), (0,)), ((), ())), preferred_e...  57.3 us
    dynamic_slice x54, local copies, waits for them, and re-layouts, on_device(): pre, _ = lax.scan(forward, start, (kernel_map, weight))  41.5 us
    dot_general x29, matrix products, spread_rows(): lax.dot_general(selector, high_part, dims, preferred_element_type=jnp.flo...  35.7 us
    dot_general x29, matrix products, spread_rows(): lax.dot_general(selector, low_part, dims, preferred_element_type=jnp.floa...  34.1 us
    dot_general x27, matrix products, offset_grads(): lax.dot_general(pre_grad, kernel, (((1,), (1,)), ((), ())), preferred_ele...  29.2 us
    all_to_all x1, waiting for transfers between devices, on_device(): lax.all_to_all(brick_grad, 'brick', split_axis=0, concat_axis=0, tiled=True)  12.8 us
  transfers between devices with their start and end apart: 8, of which 6 were waited for; matrix products, arithmetic and copies ran while one was open for 2% of the time, Pallas kernels for 0%

profile of v1, /device:TPU:0, one launch (start us, length us, event | category | flops | bytes accessed | tf_op | source)
XLA Modules:
  0.0 498.1 jit_solution(8192842222040322379)
XLA Ops:
  10.5 7.2 %all-to-all-start = ((bf16[8,128,96]{1,2,0:T(8,128)(2,1)}), bf16[8,128,96]{1,2,0:T(8,128)(2,1)S(1)}, u32[]{:S(2)}, u32[]{:S(2)}) async-start(bf16[8,128,96]{1,2,0:T(8,128)(2,1)} %bitcast.53), calls=%async_computation | async-start | bytes 393216 | tf_op jit(solution)/shard_map/all_to_all | solution.py:37
  21.3 4.4 all-to-all-done
  26.0 3.0 collective-permute-start
  30.6 4.4 collective-permute-done.1
  35.3 92.4 %while.24 = (s32[]{:T(128)}, f32[1024,256]{1,0:T(8,128)S(1)}, s32[27,1024]{1,0:T(8,128)}, bf16[1281,96]{1,0:T(8,128)(2,1)S(1)}, bf16[27,96,256]{2,1,0:T(8,128)(2,1)}, /*index=5*/s32[]{:T(128)}, s32[]{:T(128)}) while((s32[]{:T(128)}, f32[1024,256]{1,0:T(8,128)S(1)}, s32[27,1024]{1,0:T(8,128)}, bf16[1281,96]{1,0:T(8,128)(2,1)S(1)}, ...), condition=%wide.region_1.2_spmd.clone, body=%wide.region_0.1_spmd.clone.sunk | while | flops 304120832 | bytes 2404647 | solution.py:57
  36.2 2.6 convolution_add_fusion.4
  39.6 2.6 convolution_add_fusion.4
  43.0 2.6 convolution_add_fusion.4
  46.4 2.6 convolution_add_fusion.4
  49.8 2.6 convolution_add_fusion.4
  53.3 2.6 convolution_add_fusion.4
  56.7 2.6 convolution_add_fusion.4
  60.1 2.6 convolution_add_fusion.4
  63.5 2.6 convolution_add_fusion.4
  66.9 2.6 convolution_add_fusion.4
  70.4 2.6 convolution_add_fusion.4
  73.8 2.6 convolution_add_fusion.4
  77.2 2.6 convolution_add_fusion.4
  80.6 2.6 convolution_add_fusion.4
  84.0 2.6 convolution_add_fusion.4
  87.5 2.6 convolution_add_fusion.4
  90.9 2.6 convolution_add_fusion.4
  94.3 2.6 convolution_add_fusion.4
  97.7 2.6 convolution_add_fusion.4
  101.1 2.6 convolution_add_fusion.4
  104.5 2.6 convolution_add_fusion.4
  108.0 2.6 convolution_add_fusion.4
  111.4 2.6 convolution_add_fusion.4
  114.8 2.6 convolution_add_fusion.4
  118.2 2.6 convolution_add_fusion.4
  121.6 2.6 convolution_add_fusion.4
  125.1 2.6 convolution_add_fusion.4
  127.9 176.2 %while.25 = (s32[]{:T(128)}, f32[1281,96]{0,1:T(8,128)S(1)}, f32[27,96,256]{2,1,0:T(8,128)}, s32[27,1024]{1,0:T(8,128)}, bf16[27,96,256]{2,1,0:T(8,128)(2,1)}, /...) while((s32[]{:T(128)}, f32[1281,96]{0,1:T(8,128)S(1)}, ...), condition=%wide.region_3.4_spmd.clone, body=%wide.region_2.3_spmd.clone.sunk | while | flops 861121792 | bytes 4609851 | solution.py:79
  132.3 2.1 fusion.103
  138.9 2.1 fusion.103
  145.4 2.1 fusion.103
  151.9 2.1 fusion.103
  158.4 2.1 fusion.103
  165.0 2.1 fusion.103
  171.5 2.1 fusion.103
  178.0 2.1 fusion.103
  191.1 2.1 fusion.103
  304.2 59.4 %all-reduce.3.cloned.1.call-done = f32[27,96,256]{2,1,0:T(8,128)} async-done(((f32[27,96,256]{2,1,0:T(8,128)}), f32[27,96,256]{2,1,0:T(8,128)}) %all-reduce.3.cloned.1.call-update) | async-done | bytes 2654224 | tf_op jit(solution)/shard_map/psum | solution.py:80
  365.0 4.5 collective-permute-start.2
  372.7 7.2 %all-to-all-start.1 = ((bf16[8,128,96]{1,2,0:T(8,128)(2,1)}), bf16[8,128,96]{1,2,0:T(8,128)(2,1)S(1)}, u32[]{:S(2)}, u32[]{:S(2)}) async-start(bf16[8,128,96]{1,2,0:T(8,128)(2,1)} %bitcast.52), calls=%async_computation.1 | async-start | bytes 393216 | tf_op jit(solution)/shard_map/all_to_all | solution.py:91
  380.8 12.8 %all-to-all-done.1 = bf16[8,128,96]{1,2,0:T(8,128)(2,1)S(1)} async-done(((bf16[8,128,96]{1,2,0:T(8,128)(2,1)}), bf16[8,128,96]{1,2,0:T(8,128)(2,1)S(1)}, u32[]{:S(2)}, u32[]{:S(2)}) %all-to-all-start.1) | async-done | bytes 196640 | tf_op jit(solution)/shard_map/all_to_all | solution.py:91
  395.1 92.5 %all-reduce.5.cloned.1.call-done = f32[27,96,256]{2,1,0:T(8,128)} async-done(((f32[27,96,256]{2,1,0:T(8,128)}), f32[27,96,256]{2,1,0:T(8,128)}) %all-reduce.5.cloned.1.call-update) | async-done | bytes 2654224 | tf_op jit(solution)/shard_map/psum | solution.py:80
  487.6 3.6 broadcast_multiply_fusion
  (195 shorter events, 193.6 us)
Async XLA Ops:
  7.2 0.9 copy-start
  10.5 15.2 %all-to-all-start = ((bf16[8,128,96]{1,2,0:T(8,128)(2,1)}), bf16[8,128,96]{1,2,0:T(8,128)(2,1)S(1)}, u32[]{:S(2)}, u32[]{:S(2)}) async-start(bf16[8,128,96]{1,2,0:T(8,128)(2,1)} %bitcast.53), calls=%async_computation | async-start | bytes 393216 | tf_op jit(solution)/shard_map/all_to_all | solution.py:37
  17.8 345.9 %all-reduce.3.cloned.1.call-start = ((), (), s32[]{:S(2)}) async-start(), calls=%async_computation.2 | async-start | bytes 5308416 | tf_op jit(solution)/shard_map/psum | solution.py:80
  26.0 4.6 collective-permute-start
  29.3 5.7 %collective-permute-start.1 = (bf16[128,96]{0,1:T(8,128)(2,1)S(1)}, bf16[128,96]{0,1:T(8,128)(2,1)S(1)}, u32[]{:S(2)}, u32[]{:S(2)}) collective-permute-start(bf16[128,96]{0,1:T(8,128)(2,1)S(1)} %convolution_convert_fusion), channel_id=1, source_target_pairs={{4,0},{8,4},{12,8},{16,12},{20,16},{24,20},{28,24},{5,1},{9,5},{13... | collective-permute-start | bytes 73736 | tf_op jit(solution)/shard_map/ppermute | solution.py:11
  35.3 92.4 %copy-start.1 = (bf16[1024,256]{1,0:T(8,128)(2,1)S(1)}, bf16[1024,256]{1,0:T(8,128)(2,1)}, u32[]{:S(2)}) copy-start(bf16[1024,256]{1,0:T(8,128)(2,1)} %param.19) | copy-start | bytes 1572868
  35.3 92.4 %copy-start.2 = (f32[256]{0:T(256)S(1)}, f32[256]{0:T(256)}, u32[]{:S(2)}) copy-start(f32[256]{0:T(256)} %param.18) | copy-start | bytes 3076
  304.2 183.4 %all-reduce.5.cloned.1.call-start = ((), (), s32[]{:S(2)}) async-start(), calls=%async_computation.3 | async-start | bytes 5308416 | tf_op jit(solution)/shard_map/psum | solution.py:80
  363.7 5.9 %collective-permute-start.3 = (bf16[128,96]{0,1:T(8,128)(2,1)S(1)}, bf16[128,96]{0,1:T(8,128)(2,1)S(1)}, u32[]{:S(2)}, u32[]{:S(2)}) collective-permute-start(bf16[128,96]{0,1:T(8,128)(2,1)S(1)} %get-tuple-element.150), channel_id=1, source_target_pairs={{4,0},{8,4},{12,8},{16,12},{20,16},{24,20},{28,24},{5,1},{9,5},{13... | collective-permute-start | bytes 73736 | tf_op jit(solution)/shard_map/ppermute | solution.py:11
  365.0 6.1 %collective-permute-start.2 = (bf16[128,96]{0,1:T(8,128)(2,1)S(1)}, bf16[128,96]{0,1:T(8,128)(2,1)S(1)}, u32[]{:S(2)}, u32[]{:S(2)}) collective-permute-start(bf16[128,96]{0,1:T(8,128)(2,1)S(1)} %get-tuple-element.149), channel_id=1, source_target_pairs={{0,4},{4,8},{8,12},{12,16},{16,20},{20,24},{24,28},{1,5},{5,9},{9,... | collective-permute-start | bytes 73736 | tf_op jit(solution)/shard_map/ppermute | solution.py:11
  369.9 23.7 %copy-start.3 = (s32[1024]{0:T(1024)S(1)}, s32[1024]{0:T(1024)}, u32[]{:S(2)}) copy-start(s32[1024]{0:T(1024)} %param.13) | copy-start | bytes 12292
  372.7 20.9 %all-to-all-start.1 = ((bf16[8,128,96]{1,2,0:T(8,128)(2,1)}), bf16[8,128,96]{1,2,0:T(8,128)(2,1)S(1)}, u32[]{:S(2)}, u32[]{:S(2)}) async-start(bf16[8,128,96]{1,2,0:T(8,128)(2,1)} %bitcast.52), calls=%async_computation.1 | async-start | bytes 393216 | tf_op jit(solution)/shard_map/all_to_all | solution.py:91
Sparse Core Ops, SparseCore 0:
  304.3 59.3 all-reduce.2
  367.3 120.2 all-reduce.4
